TPU v7x, 256 devices: a whole 4x4x8 slice. The times are simulated.
256 devices in a mesh: seq: 64 (over z, x, core), tp: 4 (over y).
Axes of the slice: x: 4, y: 4, z: 8, core: 2. Of those that a mesh axis runs over, the one named last changes fastest.
Arguments:
- layer_input: bfloat16 [16384, 2048], P('seq'), may hold values from -1.5 to 1.5
- norm_gain: float32 [2048], replicated, may hold values from 0.5 to 1.5
- w_query: bfloat16 [2048, 2048], P(None, 'tp')
- key_weight: bfloat16 [2048, 1024], P(None, 'tp')
- value_weight: bfloat16 [2048, 1024], P(None, 'tp'), may hold values from -0.125 to 0.125
- w_out: bfloat16 [2048, 2048], P('tp'), may hold values from -1 to 1
- query_gain: float32 [128], replicated, may hold values from 0.6 to 6, as said below
- key_gain: float32 [128], replicated, may hold values from 0.6 to 6, as said below
- seg_ids: int32 [16384], P('seq'), may hold values from 0 to 7, as said below
- positions: int32 [16384], P('seq'), may hold values from 0 to 13106, as said below
- post_gain: float32 [2048], replicated, may hold values from 0.5 to 1.5
- w_gate: bfloat16 [2048, 3072], P('seq', 'tp'), may hold values from -0.125 to 0.125
- w_up: bfloat16 [2048, 3072], P('seq', 'tp'), may hold values from -0.125 to 0.125
- w_down: bfloat16 [3072, 2048], P('tp', 'seq'), may hold values from -0.21875 to 0.21875
Outputs:
- hidden: bfloat16 [16384, 2048], P('seq')
- key_cache: bfloat16 [16384, 1024], P('seq', 'tp')
- value_cache: bfloat16 [16384, 1024], P('seq', 'tp')
Inputs may be any that keep to these rules, and one draw needn't show every extreme that they name: `seg_ids`: prompt numbers never fall along the stream; each of the 8 prompts is a contiguous run of one or more tokens, and one prompt has exactly 13107 tokens. `positions`: each token's place in its prompt, counting from 0 at the prompt's first token. `query_gain`: positive gains. `key_gain`: positive gains.
All inputs are finite; a program needn't handle non-finite values.
Results may differ from a plain program's by a relative error of at most 0.02.
Values may be sent and summed in bfloat16 or wider, within the bound.
A program may use at most 128 MiB of HBM per device.

v0:
```python
import math
import jax
import jax.numpy as jnp
from jax import lax
from jax.sharding import PartitionSpec as P


def rms(v, gain):
    return v * lax.rsqrt(jnp.mean(v * v, axis=-1, keepdims=True) + 1e-06) * gain


def rope(v, place):
    half = v.shape[-1] // 2
    freqs = 1000000.0 ** (-2.0 * jnp.arange(half, dtype=jnp.float32) / v.shape[-1])
    angle = place.astype(jnp.float32)[:, None] * freqs[None, :]
    cosine = jnp.cos(angle)[:, None, :]
    sine = jnp.sin(angle)[:, None, :]
    block_start = v[..., :half]
    second = v[..., half:]
    return jnp.concatenate(
        [block_start * cosine - second * sine, second * cosine + block_start * sine], axis=-1
    )


def body(
    layer_input,
    norm_gain,
    w_query,
    key_weight,
    value_weight,
    w_out,
    query_gain,
    key_gain,
    seg_ids,
    positions,
    post_gain,
    w_gate,
    w_up,
    w_down,
):
    rows = layer_input.shape[0]
    head_size = query_gain.shape[0]
    query_local = w_query.shape[1] // head_size
    kv_local = key_weight.shape[1] // head_size
    head_group = query_local // kv_local
    scale = 1.0 / math.sqrt(head_size)
    xf = layer_input.astype(jnp.float32)
    normed_input = rms(xf, norm_gain).astype(jnp.bfloat16)
    query_matrix = jnp.dot(normed_input, w_query, preferred_element_type=jnp.float32).reshape(
        rows, query_local, head_size
    )
    query_matrix = rope(rms(query_matrix, query_gain), positions).astype(jnp.bfloat16)
    key_matrix = jnp.dot(normed_input, key_weight, preferred_element_type=jnp.float32).reshape(
        rows, kv_local, head_size
    )
    key_matrix = rope(rms(key_matrix, key_gain), positions).astype(jnp.bfloat16)
    key_cache = key_matrix.reshape(rows, kv_local * head_size)
    value_cache = jnp.dot(normed_input, value_weight, preferred_element_type=jnp.float32).astype(
        jnp.bfloat16
    )
    grouped = query_matrix.reshape(rows, kv_local, head_group, head_size).transpose(1, 2, 0, 3)
    me = lax.axis_index("seq")
    my_last = me * rows + rows - 1

    def update(state, key_rows, value_rows, seg_rows, place_rows):
        top, total, acc = state
        count = key_rows.shape[0]
        s = (
            jnp.einsum(
                "hgqd,khd->hgqk",
                grouped,
                key_rows.reshape(count, kv_local, head_size),
                preferred_element_type=jnp.float32,
            )
            * scale
        )
        allowed = (seg_ids[:, None] == seg_rows[None, :]) & (
            place_rows[None, :] <= positions[:, None]
        )
        s = jnp.where(allowed, s, -1e30)
        new_top = jnp.maximum(top, jnp.max(s, axis=-1))
        p = jnp.where(allowed, jnp.exp(s - new_top[..., None]), 0.0)
        decay = jnp.exp(top - new_top)
        total = total * decay + jnp.sum(p, axis=-1)
        acc = acc * decay[..., None] + jnp.einsum(
            "hgqk,khd->hgqd",
            p.astype(jnp.bfloat16),
            value_rows.reshape(count, kv_local, head_size),
            preferred_element_type=jnp.float32,
        )
        return (new_top, total, acc)

    start_state = (
        jnp.full((kv_local, head_group, rows), -1e30, jnp.float32),
        jnp.zeros((kv_local, head_group, rows), jnp.float32),
        jnp.zeros((kv_local, head_group, rows, head_size), jnp.float32),
    )
    travel = (key_cache, value_cache, seg_ids, positions)
    dead = jnp.int32(0) < 0
    key_rows = lax.all_gather(travel[0], "seq", axis=0, tiled=True)
    value_rows = lax.all_gather(travel[1], "seq", axis=0, tiled=True)
    seg_rows = lax.all_gather(travel[2], "seq", axis=0, tiled=True)
    place_rows = lax.all_gather(travel[3], "seq", axis=0, tiled=True)
    count = key_rows.shape[0]
    shards = count // rows
    limit = max(1, 1024 // rows)
    factor = 1
    for trial in range(1, limit + 1):
        if shards % trial == 0:
            factor = trial
    width = rows * factor

    def one_block(step, inner):
        offset = step * width
        kb = lax.dynamic_slice_in_dim(key_rows, offset, width, 0)
        vb = lax.dynamic_slice_in_dim(value_rows, offset, width, 0)
        sb = lax.dynamic_slice_in_dim(seg_rows, offset, width, 0)
        pb = lax.dynamic_slice_in_dim(place_rows, offset, width, 0)
        skip = dead | (offset > my_last) | (sb[width - 1] < seg_ids[0])
        return lax.cond(skip, lambda c: c, lambda c: update(c, kb, vb, sb, pb), inner)

    top, total, acc = lax.fori_loop(0, count // width, one_block, start_state)
    attended = (acc / total[..., None]).astype(jnp.bfloat16)
    attended = attended.transpose(2, 0, 1, 3).reshape(rows, query_local * head_size)
    partial_out = jnp.dot(attended, w_out, preferred_element_type=jnp.float32)
    summed = lax.psum(partial_out.astype(jnp.bfloat16), "tp").astype(jnp.float32)
    mid = (xf + summed).astype(jnp.bfloat16)
    mid_f = mid.astype(jnp.float32)
    post_normed = rms(mid_f, post_gain).astype(jnp.bfloat16)
    gate = jnp.dot(
        post_normed,
        lax.all_gather(w_gate, "seq", axis=0, tiled=True),
        preferred_element_type=jnp.float32,
    )
    up = jnp.dot(
        post_normed,
        lax.all_gather(w_up, "seq", axis=0, tiled=True),
        preferred_element_type=jnp.float32,
    )
    act = (jax.nn.silu(gate) * up).astype(jnp.bfloat16)
    terms = jnp.dot(
        act, lax.all_gather(w_down, "seq", axis=1, tiled=True), preferred_element_type=jnp.float32
    )
    ffn_total = lax.psum(terms.astype(jnp.bfloat16), "tp").astype(jnp.float32)
    hidden = (mid_f + ffn_total).astype(jnp.bfloat16)
    return (hidden, key_cache, value_cache)


def solution(mesh):
    in_specs = (
        P("seq", None),
        P(),
        P(None, "tp"),
        P(None, "tp"),
        P(None, "tp"),
        P("tp", None),
        P(),
        P(),
        P("seq"),
        P("seq"),
        P(),
        P("seq", "tp"),
        P("seq", "tp"),
        P("tp", "seq"),
    )
    out_specs = (P("seq", None), P("seq", "tp"), P("seq", "tp"))
    return jax.shard_map(body, mesh=mesh, in_specs=in_specs, out_specs=out_specs, check_vma=False)
```

profile of v0, /device:TPU:2, one launch (start us, length us, event | category | flops | bytes accessed | tf_op | source)
XLA Modules:
  0.0 657.9 jit_solution(4688254087747547651)
XLA Ops:
  7.3 1.6 fusion.12
  8.9 3.0 multiply_reduce_fusion.1
  12.0 0.5 multiply_cosine_fusion
  12.7 1.0 multiply_multiply_fusion.1
  13.8 0.8 copy.77
  14.6 2.4 convolution_convert_fusion.2
  17.1 3.2 fusion.28
  20.3 1.2 reshape.128
  22.2 0.5 subtract_convert_fusion
  22.8 46.4 %all-gather = s32[64,1,256]{2,1,0:T(1,128)S(1)} all-gather(s32[1,1,256]{2,1,0:T(1,128)S(1)} %bitcast.61), channel_id=1, replica_groups=mesh['seq'=64,'tp'=4] {'seq'}, dimensions={0}, use_global_device_ids=true | all-gather | bytes 66560 | tf_op jit(solution)/shard_map/all_gather | solution.py:102
  69.2 41.5 %all-gather.1 = s32[64,1,256]{2,1,0:T(1,128)S(1)} all-gather(s32[1,1,256]{2,1,0:T(1,128)S(1)} %bitcast.60), channel_id=1, replica_groups=mesh['seq'=64,'tp'=4] {'seq'}, dimensions={0}, use_global_device_ids=true | all-gather | bytes 66560 | tf_op jit(solution)/shard_map/all_gather | solution.py:103
  110.9 11.9 %copy.67 = bf16[16384,256]{0,1:T(8,128)(2,1)} copy(bf16[16384,256]{1,0:T(8,128)(2,1)} %all-gather.8.cloned.1.call-done) | data formatting | bytes 16777216 | tf_op jit(solution)/shard_map/while | solution.py:122
  122.8 60.4 %all-gather.10.cloned.1.call-done = bf16[16384,256]{1,0:T(8,128)(2,1)} async-done(((bf16[256,256]{1,0:T(8,128)(2,1)}), bf16[16384,256]{1,0:T(8,128)(2,1)}) %all-gather.10.cloned.1.call-update) | async-done | bytes 8388624 | tf_op jit(solution)/shard_map/all_gather | solution.py:101
  183.2 11.8 %copy.68 = bf16[16384,256]{0,1:T(8,128)(2,1)} copy(bf16[16384,256]{1,0:T(8,128)(2,1)} %all-gather.10.cloned.1.call-done) | data formatting | bytes 16777216 | tf_op jit(solution)/shard_map/while | solution.py:122
  195.0 44.5 %while.17 = (s32[]{:T(128)}, f32[2,2,256]{2,1,0:T(2,128)S(1)}, f32[2,2,256]{2,1,0:T(2,128)S(1)}, f32[2,2,256,128]{3,2,1,0:T(8,128)S(1)}, s32[]{:T(128)}, /*index...) while((s32[]{:T(128)}, f32[2,2,256]{2,1,0:T(2,128)S(1)}, ...), condition=%wide.region_8.9_spmd, body=%wide.region_3.8_spmd.sunk | while | flops 551553024 | bytes 18180480 | solution.py:122
  195.1 0.6 slice.44
  195.7 0.5 slice.45
  197.4 5.3 conditional.2
  197.8 1.3 constant_dynamic-slice_fusion
  199.1 0.9 fusion
  200.0 1.0 fusion.2
  201.1 1.6 fusion.6
  202.8 0.6 slice.44
  203.4 0.5 slice.45
  205.2 0.6 slice.44
  205.9 0.5 slice.45
  207.7 0.6 slice.44
  208.3 0.5 slice.45
  210.1 0.6 slice.44
  210.8 0.5 slice.45
  212.6 0.6 slice.44
  213.2 0.5 slice.45
  215.1 0.6 slice.44
  215.7 0.5 slice.45
  217.5 0.6 slice.44
  218.2 0.5 slice.45
  220.0 0.6 slice.44
  220.6 0.5 slice.45
  222.4 0.6 slice.44
  223.1 0.5 slice.45
  224.9 0.6 slice.44
  225.5 0.5 slice.45
  227.3 0.6 slice.44
  228.0 0.5 slice.45
  229.8 0.6 slice.44
  230.4 0.5 slice.45
  232.2 0.6 slice.44
  234.7 0.6 slice.44
  235.3 0.5 slice.45
  237.1 0.6 slice.44
  237.8 0.5 slice.45
  239.8 1.7 convolution_convert_fusion
  241.6 0.5 all-gather.12.cloned.1.call-update
  242.2 0.5 all-gather.14.cloned.1.call-update
  242.8 0.5 all-gather.16.cloned.1.call-update
  243.5 110.3 %all-reduce.3.cloned.1.call-done = bf16[256,2048]{1,0:T(8,128)(2,1)} async-done(((bf16[256,2048]{1,0:T(8,128)(2,1)}), bf16[256,2048]{1,0:T(8,128)(2,1)}) %all-reduce.3.cloned.1.call-update) | async-done | bytes 1048592 | tf_op jit(solution)/shard_map/psum | solution.py:126
  353.8 2.0 fusion.16
  355.9 78.9 %all-gather.12.cloned.1.call-done = bf16[2048,768]{1,0:T(8,128)(2,1)} async-done(((bf16[32,768]{1,0:T(8,128)(2,1)}), bf16[2048,768]{1,0:T(8,128)(2,1)}) %all-gather.12.cloned.1.call-update) | async-done | bytes 3145744 | tf_op jit(solution)/shard_map/all_gather | solution.py:132
  434.8 3.8 fusion.24
  438.6 75.0 %all-gather.14.cloned.1.call-done = bf16[2048,768]{1,0:T(8,128)(2,1)} async-done(((bf16[32,768]{1,0:T(8,128)(2,1)}), bf16[2048,768]{1,0:T(8,128)(2,1)}) %all-gather.14.cloned.1.call-update) | async-done | bytes 3145744 | tf_op jit(solution)/shard_map/all_gather | solution.py:137
  513.6 78.8 %all-gather.16.cloned.1.call-done = bf16[768,2048]{0,1:T(8,128)(2,1)} async-done(((bf16[768,32]{0,1:T(8,128)(2,1)}), bf16[768,2048]{0,1:T(8,128)(2,1)}) %all-gather.16.cloned.1.call-update) | async-done | bytes 3145744 | tf_op jit(solution)/shard_map/all_gather | solution.py:142
  592.4 6.2 convolution_convert_fusion.1
  598.7 49.8 %all-reduce.5.cloned.1.call-done = bf16[256,2048]{1,0:T(8,128)(2,1)} async-done(((bf16[256,2048]{1,0:T(8,128)(2,1)}), bf16[256,2048]{1,0:T(8,128)(2,1)}) %all-reduce.5.cloned.1.call-update) | async-done | bytes 1048592 | tf_op jit(solution)/shard_map/psum | solution.py:144
  648.5 2.6 fusion.19
  (113 shorter events, 3.6 us)
Async XLA Ops:
  7.2 232.6 %copy-start = (bf16[512,2048]{1,0:T(8,128)(2,1)S(1)}, bf16[512,2048]{1,0:T(8,128)(2,1)}, u32[]{:S(2)}) copy-start(bf16[512,2048]{1,0:T(8,128)(2,1)} %param.23) | copy-start | bytes 6291460
  7.2 4.8 copy-start.2
  7.2 103.7 %all-gather.8.cloned.1.call-start = ((), (), s32[]{:S(2)}) async-start(), calls=%async_computation | async-start | bytes 8519680 | tf_op jit(solution)/shard_map/all_gather | solution.py:100
  8.9 3.8 copy-start.4
  8.9 5.7 copy-start.1
  14.6 168.6 %all-gather.10.cloned.1.call-start = ((), (), s32[]{:S(2)}) async-start(), calls=%async_computation.1 | async-start | bytes 8519680 | tf_op jit(solution)/shard_map/all_gather | solution.py:101
  17.0 336.8 %all-reduce.3.cloned.1.call-start = ((), (), s32[]{:S(2)}) async-start(), calls=%async_computation.2 | async-start | bytes 2097152 | tf_op jit(solution)/shard_map/psum | solution.py:126
  17.1 4.8 copy-start.5
  21.9 1.0 copy-start.3
  241.5 193.3 %copy-start.6 = (f32[2048]{0:T(1024)S(1)}, f32[2048]{0:T(1024)}, u32[]{:S(2)}) copy-start(f32[2048]{0:T(1024)} %param.28) | copy-start | bytes 24580
  241.5 193.3 %all-gather.12.cloned.1.call-start = ((), (), s32[]{:S(2)}) async-start(), calls=%async_computation.3 | async-start | bytes 3194880 | tf_op jit(solution)/shard_map/all_gather | solution.py:132
  242.1 271.5 %all-gather.14.cloned.1.call-start = ((), (), s32[]{:S(2)}) async-start(), calls=%async_computation.4 | async-start | bytes 3194880 | tf_op jit(solution)/shard_map/all_gather | solution.py:137
  242.7 349.7 %all-gather.16.cloned.1.call-start = ((), (), s32[]{:S(2)}) async-start(), calls=%async_computation.5 | async-start | bytes 3194880 | tf_op jit(solution)/shard_map/all_gather | solution.py:142
  243.3 405.2 %all-reduce.5.cloned.1.call-start = ((), (), s32[]{:S(2)}) async-start(), calls=%async_computation.6 | async-start | bytes 2097152 | tf_op jit(solution)/shard_map/psum | solution.py:144
Sparse Core Ops, SparseCore 0:
  14.7 84.7 all-gather.7
  102.8 80.3 all-gather.9
  241.7 112.1 all-reduce.2
  356.8 77.9 all-gather.11
  437.8 75.7 all-gather.13
  516.6 75.7 all-gather.15
  598.8 49.6 all-reduce.4
where the time goes:
time: 659 us; the launch traced here: 658 us
  waiting for transfers between devices  455 us (69%)
  blocking collectives  87.9 us (13%)
  local copies, waits for them, and re-layouts  45.7 us (7%)
  matrix products  22.9 us (3%)
  loops' own time  21 us (3%)
  between operations  14.4 us (2%)
  other arithmetic  10.7 us (2%)
    psum x1, waiting for transfers between devices, body(): lax.psum(partial_out.astype(jnp.bfloat16), 'tp').astype(jnp.float32)  110 us
    all_gather x1, waiting for transfers between devices, body(): lax.all_gather(w_gate, 'seq', axis=0, tiled=True)  78.9 us
    all_gather x1, waiting for transfers between devices, body(): lax.all_gather(w_down, 'seq', axis=1, tiled=True)  78.8 us
    all_gather x1, waiting for transfers between devices, body(): lax.all_gather(w_up, 'seq', axis=0, tiled=True)  75 us
    all_gather x1, waiting for transfers between devices, body(): value_rows = lax.all_gather(travel[1], 'seq', axis=0, tiled=True)  60.4 us
    psum x1, waiting for transfers between devices, body(): ffn_total = lax.psum(terms.astype(jnp.bfloat16), 'tp').astype(jnp.float32)  49.8 us
    all_gather x1, blocking collectives, body(): seg_rows = lax.all_gather(travel[2], 'seq', axis=0, tiled=True)  46.4 us
    all_gather x1, blocking collectives, body(): place_rows = lax.all_gather(travel[3], 'seq', axis=0, tiled=True)  41.5 us
  transfers between devices with their start and end apart: 7, of which 6 were waited for; matrix products, arithmetic and copies ran while one was open for 4% of the time, Pallas kernels for 0%

commit v1 on v0

--- a/solution.py
+++ b/solution.py
@@ -3,6 +3,10 @@
 import jax.numpy as jnp
 from jax import lax
 from jax.sharding import PartitionSpec as P
+
+
+def tell_links(inp):
+    return lax.all_gather(inp, "tp").sum(axis=0)
 
 
 def rms(v, gain):
@@ -123,7 +127,7 @@
     attended = (acc / total[..., None]).astype(jnp.bfloat16)
     attended = attended.transpose(2, 0, 1, 3).reshape(rows, query_local * head_size)
     partial_out = jnp.dot(attended, w_out, preferred_element_type=jnp.float32)
-    summed = lax.psum(partial_out.astype(jnp.bfloat16), "tp").astype(jnp.float32)
+    summed = tell_links(partial_out.astype(jnp.bfloat16)).astype(jnp.float32)
     mid = (xf + summed).astype(jnp.bfloat16)
     mid_f = mid.astype(jnp.float32)
     post_normed = rms(mid_f, post_gain).astype(jnp.bfloat16)

time: 659 us -> 658 us (level)
    psum x1 -> x0, waiting for transfers between devices: 110 us -> none  [body(): lax.psum(partial_out.astype(jnp.bfloat16), 'tp').astype(jnp.float32)]
    all_gather x0 -> x1, waiting for transfers between devices: none -> 110 us  [tell_links(): return lax.all_gather(inp, 'tp').sum(axis=0)]
  transfers between devices with their start and end apart: 7 -> 7, of which waited for: 6 -> 6; matrix products, arithmetic and copies ran while one was open for 4% -> 5% of each run, Pallas kernels for 0% -> 0%
where the time goes in v1:
time: 658 us; the launch traced here: 656 us
  waiting for transfers between devices  449 us (68%)
  blocking collectives  87.9 us (13%)
  local copies, waits for them, and re-layouts  45.7 us (7%)
  matrix products  22.8 us (3%)
  loops' own time  21 us (3%)
  other arithmetic  15 us (2%)
  between operations  14.4 us (2%)
    all_gather x1, waiting for transfers between devices, tell_links(): return lax.all_gather(inp, 'tp').sum(axis=0)  110 us
    all_gather x1, waiting for transfers between devices, body(): lax.all_gather(w_down, 'seq', axis=1, tiled=True)  78.4 us
    all_gather x1, waiting for transfers between devices, body(): lax.all_gather(w_up, 'seq', axis=0, tiled=True)  74.6 us
    all_gather x1, waiting for transfers between devices, body(): lax.all_gather(w_gate, 'seq', axis=0, tiled=True)  73.8 us
    all_gather x1, waiting for transfers between devices, body(): value_rows = lax.all_gather(travel[1], 'seq', axis=0, tiled=True)  60.4 us
    psum x1, waiting for transfers between devices, body(): ffn_total = lax.psum(terms.astype(jnp.bfloat16), 'tp').astype(jnp.float32)  49.8 us
    all_gather x1, blocking collectives, body(): seg_rows = lax.all_gather(travel[2], 'seq', axis=0, tiled=True)  46.4 us
    all_gather x1, blocking collectives, body(): place_rows = lax.all_gather(travel[3], 'seq', axis=0, tiled=True)  41.5 us
  transfers between devices with their start and end apart: 7, of which 6 were waited for; matrix products, arithmetic and copies ran while one was open for 5% of the time, Pallas kernels for 0%

profile of v1, /device:TPU:2, one launch (start us, length us, event | category | flops | bytes accessed | tf_op | source)
XLA Modules:
  0.0 656.1 jit_solution(5143650675948523525)
XLA Ops:
  7.3 1.7 fusion.12
  8.9 2.9 multiply_reduce_fusion.1
  11.9 0.5 multiply_cosine_fusion
  12.6 1.0 multiply_multiply_fusion.1
  13.7 0.8 copy.77
  14.6 2.4 convolution_convert_fusion.2
  17.0 3.2 fusion.28
  20.2 1.2 reshape.128
  22.2 0.5 subtract_convert_fusion
  22.8 46.4 %all-gather.1 = s32[64,1,256]{2,1,0:T(1,128)S(1)} all-gather(s32[1,1,256]{2,1,0:T(1,128)S(1)} %bitcast.63), channel_id=1, replica_groups=mesh['seq'=64,'tp'=4] {'seq'}, dimensions={0}, use_global_device_ids=true | all-gather | bytes 66560 | tf_op jit(solution)/shard_map/all_gather | solution.py:106
  69.2 41.5 %all-gather.2 = s32[64,1,256]{2,1,0:T(1,128)S(1)} all-gather(s32[1,1,256]{2,1,0:T(1,128)S(1)} %bitcast.62), channel_id=1, replica_groups=mesh['seq'=64,'tp'=4] {'seq'}, dimensions={0}, use_global_device_ids=true | all-gather | bytes 66560 | tf_op jit(solution)/shard_map/all_gather | solution.py:107
  110.8 11.9 %copy.67 = bf16[16384,256]{0,1:T(8,128)(2,1)} copy(bf16[16384,256]{1,0:T(8,128)(2,1)} %all-gather.10.cloned.1.call-done) | data formatting | bytes 16777216 | tf_op jit(solution)/shard_map/while | solution.py:126
  122.7 60.4 %all-gather.12.cloned.1.call-done = bf16[16384,256]{1,0:T(8,128)(2,1)} async-done(((bf16[256,256]{1,0:T(8,128)(2,1)}), bf16[16384,256]{1,0:T(8,128)(2,1)}) %all-gather.12.cloned.1.call-update) | async-done | bytes 8388624 | tf_op jit(solution)/shard_map/all_gather | solution.py:105
  183.1 11.8 %copy.68 = bf16[16384,256]{0,1:T(8,128)(2,1)} copy(bf16[16384,256]{1,0:T(8,128)(2,1)} %all-gather.12.cloned.1.call-done) | data formatting | bytes 16777216 | tf_op jit(solution)/shard_map/while | solution.py:126
  194.9 44.5 %while.17 = (s32[]{:T(128)}, f32[2,2,256]{2,1,0:T(2,128)S(1)}, f32[2,2,256]{2,1,0:T(2,128)S(1)}, f32[2,2,256,128]{3,2,1,0:T(8,128)S(1)}, s32[]{:T(128)}, /*index...) while((s32[]{:T(128)}, f32[2,2,256]{2,1,0:T(2,128)S(1)}, ...), condition=%wide.region_8.9_spmd, body=%wide.region_3.8_spmd.sunk | while | flops 551553024 | bytes 18180480 | solution.py:126
  195.0 0.6 slice.44
  195.6 0.5 slice.45
  197.3 5.3 conditional.2
  197.7 1.3 constant_dynamic-slice_fusion
  199.0 0.9 fusion
  200.0 1.0 fusion.2
  201.0 1.6 fusion.6
  202.7 0.6 slice.44
  203.4 0.5 slice.45
  205.2 0.6 slice.44
  205.8 0.5 slice.45
  207.6 0.6 slice.44
  208.3 0.5 slice.45
  210.1 0.6 slice.44
  210.7 0.5 slice.45
  212.5 0.6 slice.44
  213.2 0.5 slice.45
  215.0 0.6 slice.44
  215.6 0.5 slice.45
  217.4 0.6 slice.44
  218.1 0.5 slice.45
  219.9 0.6 slice.44
  220.5 0.5 slice.45
  222.3 0.6 slice.44
  223.0 0.5 slice.45
  224.8 0.6 slice.44
  225.4 0.5 slice.45
  227.2 0.6 slice.44
  227.9 0.5 slice.45
  229.7 0.6 slice.44
  232.1 0.6 slice.44
  234.6 0.6 slice.44
  235.2 0.5 slice.45
  237.1 0.6 slice.44
  237.7 0.5 slice.45
  239.7 1.7 convolution_convert_fusion
  241.5 0.5 all-gather.14.cloned.1.call-update
  242.1 0.5 all-gather.16.cloned.1.call-update
  242.7 0.5 all-gather.18.cloned.1.call-update
  243.4 110.2 %all-gather.20.cloned.1.call-done = bf16[1024,2048]{1,0:T(8,128)(2,1)} async-done(((bf16[256,2048]{1,0:T(8,128)(2,1)}), bf16[1024,2048]{1,0:T(8,128)(2,1)}) %all-gather.20.cloned.1.call-update) | async-done | bytes 4194320 | tf_op jit(solution)/shard_map/all_gather | solution.py:9
  353.7 4.2 reduce_sum.62
  357.9 2.0 fusion.16
  360.0 73.8 %all-gather.14.cloned.1.call-done = bf16[2048,768]{1,0:T(8,128)(2,1)} async-done(((bf16[32,768]{1,0:T(8,128)(2,1)}), bf16[2048,768]{1,0:T(8,128)(2,1)}) %all-gather.14.cloned.1.call-update) | async-done | bytes 3145744 | tf_op jit(solution)/shard_map/all_gather | solution.py:136
  433.8 3.8 fusion.24
  437.6 74.6 %all-gather.16.cloned.1.call-done = bf16[2048,768]{1,0:T(8,128)(2,1)} async-done(((bf16[32,768]{1,0:T(8,128)(2,1)}), bf16[2048,768]{1,0:T(8,128)(2,1)}) %all-gather.16.cloned.1.call-update) | async-done | bytes 3145744 | tf_op jit(solution)/shard_map/all_gather | solution.py:141
  512.2 78.4 %all-gather.18.cloned.1.call-done = bf16[768,2048]{0,1:T(8,128)(2,1)} async-done(((bf16[768,32]{0,1:T(8,128)(2,1)}), bf16[768,2048]{0,1:T(8,128)(2,1)}) %all-gather.18.cloned.1.call-update) | async-done | bytes 3145744 | tf_op jit(solution)/shard_map/all_gather | solution.py:146
  590.6 6.2 convolution_convert_fusion.1
  596.9 49.8 %all-reduce.2.cloned.1.call-done = bf16[256,2048]{1,0:T(8,128)(2,1)} async-done(((bf16[256,2048]{1,0:T(8,128)(2,1)}), bf16[256,2048]{1,0:T(8,128)(2,1)}) %all-reduce.2.cloned.1.call-update) | async-done | bytes 1048592 | tf_op jit(solution)/shard_map/psum | solution.py:148
  646.6 2.6 fusion.19
  (114 shorter events, 4.0 us)
Async XLA Ops:
  7.2 232.6 %copy-start = (bf16[512,2048]{1,0:T(8,128)(2,1)S(1)}, bf16[512,2048]{1,0:T(8,128)(2,1)}, u32[]{:S(2)}) copy-start(bf16[512,2048]{1,0:T(8,128)(2,1)} %param.23) | copy-start | bytes 6291460
  7.2 4.7 copy-start.2
  7.2 5.4 copy-start.4
  7.2 103.6 %all-gather.10.cloned.1.call-start = ((), (), s32[]{:S(2)}) async-start(), calls=%async_computation | async-start | bytes 8519680 | tf_op jit(solution)/shard_map/all_gather | solution.py:104
  7.3 7.3 %copy-start.1 = (bf16[256,2048]{1,0:T(8,128)(2,1)S(1)}, bf16[256,2048]{1,0:T(8,128)(2,1)}, u32[]{:S(2)}) copy-start(bf16[256,2048]{1,0:T(8,128)(2,1)} %param.18) | copy-start | bytes 3145732
  14.5 168.6 %all-gather.12.cloned.1.call-start = ((), (), s32[]{:S(2)}) async-start(), calls=%async_computation.1 | async-start | bytes 8519680 | tf_op jit(solution)/shard_map/all_gather | solution.py:105
  17.0 336.7 %all-gather.20.cloned.1.call-start = ((), (), s32[]{:S(2)}) async-start(), calls=%async_computation.6 | async-start | bytes 5242880 | tf_op jit(solution)/shard_map/all_gather | solution.py:9
  17.0 4.8 copy-start.5
  20.2 2.6 copy-start.3
  241.5 192.3 %all-gather.14.cloned.1.call-start = ((), (), s32[]{:S(2)}) async-start(), calls=%async_computation.2 | async-start | bytes 3194880 | tf_op jit(solution)/shard_map/all_gather | solution.py:136
  242.0 270.1 %all-gather.16.cloned.1.call-start = ((), (), s32[]{:S(2)}) async-start(), calls=%async_computation.3 | async-start | bytes 3194880 | tf_op jit(solution)/shard_map/all_gather | solution.py:141
  242.6 348.0 %all-gather.18.cloned.1.call-start = ((), (), s32[]{:S(2)}) async-start(), calls=%async_computation.4 | async-start | bytes 3194880 | tf_op jit(solution)/shard_map/all_gather | solution.py:146
  243.2 403.4 %all-reduce.2.cloned.1.call-start = ((), (), s32[]{:S(2)}) async-start(), calls=%async_computation.5 | async-start | bytes 2097152 | tf_op jit(solution)/shard_map/psum | solution.py:148
  353.7 80.1 %copy-start.6 = (f32[2048]{0:T(1024)S(1)}, f32[2048]{0:T(1024)}, u32[]{:S(2)}) copy-start(f32[2048]{0:T(1024)} %param.28) | copy-start | bytes 24580
Sparse Core Ops, SparseCore 0:
  14.6 84.7 all-gather.9
  102.7 80.3 all-gather.11
  241.6 112.0 all-gather.19
  356.3 77.4 all-gather.13
  436.4 75.7 all-gather.15
  514.8 75.7 all-gather.17
  597.0 49.5 all-reduce.1
